TPU v7x, 32 devices: a whole 2x2x4 slice. The times are simulated.
32 devices in a mesh: samp: 32 (over z, y, x, core).
Axes of the slice: x: 2, y: 2, z: 4, core: 2. Of those that a mesh axis runs over, the one named last changes fastest.
Arguments:
- inputs: float32 [30, 65536], P(None, 'samp'), may hold values from -1 to 1
- response: float32 [32, 65536], P(None, 'samp')
- multi_index: int32 [5456, 30], replicated, may hold values from 0 to 3, as said below
- chosen: int32 [3], replicated, may hold values from 0 to 5455, as said below
Outputs:
- residual: float32 [32, 65536], P(None, 'samp')
- correlations: float32 [3, 32, 5456], replicated
- coefficients: float32 [3, 32], replicated
Inputs may be any that keep to these rules, and one draw needn't show every extreme that they name: `multi_index`: rows are distinct; each row's degrees sum to 3 or less. `chosen`: distinct indices.
All inputs are finite; a program needn't handle non-finite values. Where the computation divides by a largest or mean magnitude, that divisor is 1e-20 or more.
Results may differ from a plain program's by a relative error of at most 0.0062.
Values sent between devices are 32-bit elements; how exact they have to be, the bound alone decides.
A program may use at most 128 MiB of HBM per device.

v0:
```python
import math

import jax
import jax.numpy as jnp
from jax import lax
from jax.sharding import PartitionSpec as P


def factor_table(inputs):
    one = jnp.ones_like(inputs)
    second = (3.0 * inputs * inputs - 1.0) * 0.5
    third = (5.0 * inputs * inputs * inputs - 3.0 * inputs) * 0.5
    stacked = jnp.stack(
        [one, inputs * math.sqrt(3.0), second * math.sqrt(5.0), third * math.sqrt(7.0)], axis=1
    )
    return stacked.reshape(inputs.shape[0] * 4, inputs.shape[1])


def slot_index(multi_index):
    count = multi_index.shape[1]
    positive = multi_index > 0
    rank = jnp.cumsum(positive.astype(jnp.int32), axis=1) - 1
    flat_pos = jnp.arange(count, dtype=jnp.int32)[None, :] * 4 + multi_index
    result = []
    for slot in range(3):
        picked = jnp.logical_and(positive, rank == slot)
        result.append(jnp.sum(jnp.where(picked, flat_pos, 0), axis=1))
    return tuple(result)


def design(flat, index):
    first = jnp.take(flat, index[0], axis=0)
    second = jnp.take(flat, index[1], axis=0)
    third = jnp.take(flat, index[2], axis=0)
    return (first * second * third).astype(jnp.bfloat16)


def selectors(index, levels):
    columns = jnp.arange(levels, dtype=jnp.int32)[None, :]
    return tuple(((i[:, None] == columns).astype(jnp.float32) for i in index))


def design_select(piece, picks):
    first = jnp.dot(picks[0], piece, precision=lax.Precision.HIGHEST)
    second = jnp.dot(picks[1], piece, precision=lax.Precision.HIGHEST)
    third = jnp.dot(picks[2], piece, precision=lax.Precision.HIGHEST)
    return (first * second * third).astype(jnp.bfloat16)


def on_device(inputs, response, multi_index, chosen):
    rows = inputs.shape[1]
    devices = lax.axis_size("samp")
    samples = rows * devices
    cands = multi_index.shape[0]
    iters = chosen.shape[0]
    resp = response.shape[0]
    flat = factor_table(inputs)
    index = slot_index(multi_index)
    active = design(flat, tuple((i[chosen] for i in index)))
    gram_local = jnp.dot(active, active.T, preferred_element_type=jnp.float32)
    gram = lax.psum(gram_local, "samp")
    picks = selectors(index, flat.shape[0])
    width = math.gcd(rows, 512)
    nblocks = rows // width

    def build(i, table):
        piece = lax.dynamic_slice_in_dim(flat, i * width, width, 1)
        return lax.dynamic_update_slice_in_dim(table, design_select(piece, picks), i * width, 1)

    basis = lax.fori_loop(0, nblocks, build, jnp.zeros((cands, rows), jnp.bfloat16))
    residual = response
    coefs = jnp.zeros((iters, resp), jnp.float32)
    outs = []
    for k in range(iters):
        rb = residual.astype(jnp.bfloat16)
        corr_local = lax.dot_general(
            rb, basis, (((1,), (1,)), ((), ())), preferred_element_type=jnp.float32
        )
        sq_local = jnp.sum(residual * residual, axis=1)
        packed = jnp.concatenate([corr_local, sq_local[:, None]], axis=1)
        total = lax.psum(packed, "samp")
        corr = total[:, :cands]
        largest = jnp.max(jnp.abs(corr), axis=1)
        sq = total[:, cands]
        norm = math.sqrt(samples) * jnp.sqrt(sq / samples + 1e-06)
        outs.append(corr / norm[:, None])
        gamma = jnp.abs(corr[:, chosen[k]]) / (largest + 1e-06)
        factor = jnp.linalg.cholesky(gram[: k + 1, : k + 1])
        target = corr[:, chosen[: k + 1]].T
        weights = jax.scipy.linalg.cho_solve((factor, True), target)
        update = jnp.dot(
            weights.T, active[: k + 1].astype(jnp.float32), precision=lax.Precision.HIGHEST
        )
        residual = residual - gamma[:, None] * update
        coefs = coefs.at[: k + 1].add(weights * gamma[None, :])
    return (residual, jnp.stack(outs), coefs)


def solution(mesh):
    placed = (P(None, "samp"), P(None, "samp"), P(), P())
    return jax.shard_map(
        on_device,
        mesh=mesh,
        in_specs=placed,
        out_specs=(P(None, "samp"), P(), P()),
        check_vma=False,
    )
```

profile of v0, /device:TPU:0, one launch (start us, length us, event | category | flops | bytes accessed | tf_op | source)
XLA Modules:
  0.0 602.6 jit_solution(1658574804893128732)
XLA Ops:
  7.2 1.1 multiply_reduce_fusion.2
  8.4 1.0 multiply_bitcast_fusion
  9.6 0.6 copy.22
  10.6 1.2 fusion.24
  12.4 1.8 select_reduce_fusion.2
  14.2 7.7 %broadcast_in_dim.27 = bf16[5456,2048]{1,0:T(8,128)(2,1)} broadcast(bf16[]{:T(256)} %constant.269.clone.1), dimensions={} | broadcast | bytes 22347778 | tf_op jit(solution)/shard_map/broadcast_in_dim | solution.py:70
  21.8 124.4 %while.19 = (s32[]{:T(128)}, bf16[5456,2048]{1,0:T(8,128)(2,1)}, f32[120,2048]{1,0:T(8,128)S(1)}, s32[5456]{0:T(1024)S(1)}, s32[5456]{0:T(1024)S(1)}, /*index=5*...) while((s32[]{:T(128)}, bf16[5456,2048]{1,0:T(8,128)(2,1)}, ...), condition=%wide.region_5.6_spmd.clone, body=%wide.region_4.5_spmd.clone.sunk | while | flops 12080107520 | bytes 51094688 | solution.py:70
  21.8 9.2 %fusion.100 = f32[512,5456]{0,1:T(8,128)S(1)} fusion(s32[5456]{0:T(1024)S(1)} %get-tuple-element.295, f32[120,2048]{1,0:T(8,128)S(1)} %get-tuple-element.294, s32[]{:T(128)S(6)} %select_n.104), kind=kOutput, calls=%fused_computation.19.clone.1 | convolution fusion | flops 4023909120 | bytes 11444228 | tf_op jit(solution)/shard_map/while/body/eval_jaxpr/dot_general | solution.py:44
  31.1 9.3 %fusion.101 = f32[512,5456]{0,1:T(8,128)S(1)} fusion(s32[5456]{0:T(1024)S(1)} %get-tuple-element.296, f32[120,2048]{1,0:T(8,128)S(1)} %get-tuple-element.294, s32[]{:T(128)S(6)} %select_n.104), kind=kOutput, calls=%fused_computation.16.clone.1 | convolution fusion | flops 4023909120 | bytes 11444228 | tf_op jit(solution)/shard_map/while/body/eval_jaxpr/dot_general | solution.py:45
  40.3 12.6 %fusion.102 = bf16[5456,2048]{1,0:T(8,128)(2,1)} fusion(bf16[5456,2048]{1,0:T(8,128)(2,1)} %get-tuple-element.283, s32[]{:T(128)S(6)} %select_n.104, f32[512,5456]{0,1:T(8,128)S(1)} %fusion.100, f32[512,5456]{0,1:T(8,128)S(1)} %fusion.101, s32[5456]{0:T(1024)S(1)} %get-tuple-element.297, f32[120,2048]{1,0:T(8,128)S(1)} %get-tuple-element.294), kind=kOutput, calls=%fused_computation.13.clone.1 | convolution fusion | flops 4032289536 | bytes 28206080 | tf_op jit(solution)/shard_map/while/body/eval_jaxpr/dot_general | solution.py:46
  52.9 9.2 %fusion.100 = f32[512,5456]{0,1:T(8,128)S(1)} fusion(s32[5456]{0:T(1024)S(1)} %get-tuple-element.295, f32[120,2048]{1,0:T(8,128)S(1)} %get-tuple-element.294, s32[]{:T(128)S(6)} %select_n.104), kind=kOutput, calls=%fused_computation.19.clone.1 | convolution fusion | flops 4023909120 | bytes 11444228 | tf_op jit(solution)/shard_map/while/body/eval_jaxpr/dot_general | solution.py:44
  62.2 9.3 %fusion.101 = f32[512,5456]{0,1:T(8,128)S(1)} fusion(s32[5456]{0:T(1024)S(1)} %get-tuple-element.296, f32[120,2048]{1,0:T(8,128)S(1)} %get-tuple-element.294, s32[]{:T(128)S(6)} %select_n.104), kind=kOutput, calls=%fused_computation.16.clone.1 | convolution fusion | flops 4023909120 | bytes 11444228 | tf_op jit(solution)/shard_map/while/body/eval_jaxpr/dot_general | solution.py:45
  71.4 12.6 %fusion.102 = bf16[5456,2048]{1,0:T(8,128)(2,1)} fusion(bf16[5456,2048]{1,0:T(8,128)(2,1)} %get-tuple-element.283, s32[]{:T(128)S(6)} %select_n.104, f32[512,5456]{0,1:T(8,128)S(1)} %fusion.100, f32[512,5456]{0,1:T(8,128)S(1)} %fusion.101, s32[5456]{0:T(1024)S(1)} %get-tuple-element.297, f32[120,2048]{1,0:T(8,128)S(1)} %get-tuple-element.294), kind=kOutput, calls=%fused_computation.13.clone.1 | convolution fusion | flops 4032289536 | bytes 28206080 | tf_op jit(solution)/shard_map/while/body/eval_jaxpr/dot_general | solution.py:46
  84.0 9.2 %fusion.100 = f32[512,5456]{0,1:T(8,128)S(1)} fusion(s32[5456]{0:T(1024)S(1)} %get-tuple-element.295, f32[120,2048]{1,0:T(8,128)S(1)} %get-tuple-element.294, s32[]{:T(128)S(6)} %select_n.104), kind=kOutput, calls=%fused_computation.19.clone.1 | convolution fusion | flops 4023909120 | bytes 11444228 | tf_op jit(solution)/shard_map/while/body/eval_jaxpr/dot_general | solution.py:44
  93.3 9.3 %fusion.101 = f32[512,5456]{0,1:T(8,128)S(1)} fusion(s32[5456]{0:T(1024)S(1)} %get-tuple-element.296, f32[120,2048]{1,0:T(8,128)S(1)} %get-tuple-element.294, s32[]{:T(128)S(6)} %select_n.104), kind=kOutput, calls=%fused_computation.16.clone.1 | convolution fusion | flops 4023909120 | bytes 11444228 | tf_op jit(solution)/shard_map/while/body/eval_jaxpr/dot_general | solution.py:45
  102.5 12.6 %fusion.102 = bf16[5456,2048]{1,0:T(8,128)(2,1)} fusion(bf16[5456,2048]{1,0:T(8,128)(2,1)} %get-tuple-element.283, s32[]{:T(128)S(6)} %select_n.104, f32[512,5456]{0,1:T(8,128)S(1)} %fusion.100, f32[512,5456]{0,1:T(8,128)S(1)} %fusion.101, s32[5456]{0:T(1024)S(1)} %get-tuple-element.297, f32[120,2048]{1,0:T(8,128)S(1)} %get-tuple-element.294), kind=kOutput, calls=%fused_computation.13.clone.1 | convolution fusion | flops 4032289536 | bytes 28206080 | tf_op jit(solution)/shard_map/while/body/eval_jaxpr/dot_general | solution.py:46
  115.1 9.2 %fusion.100 = f32[512,5456]{0,1:T(8,128)S(1)} fusion(s32[5456]{0:T(1024)S(1)} %get-tuple-element.295, f32[120,2048]{1,0:T(8,128)S(1)} %get-tuple-element.294, s32[]{:T(128)S(6)} %select_n.104), kind=kOutput, calls=%fused_computation.19.clone.1 | convolution fusion | flops 4023909120 | bytes 11444228 | tf_op jit(solution)/shard_map/while/body/eval_jaxpr/dot_general | solution.py:44
  124.3 9.3 %fusion.101 = f32[512,5456]{0,1:T(8,128)S(1)} fusion(s32[5456]{0:T(1024)S(1)} %get-tuple-element.296, f32[120,2048]{1,0:T(8,128)S(1)} %get-tuple-element.294, s32[]{:T(128)S(6)} %select_n.104), kind=kOutput, calls=%fused_computation.16.clone.1 | convolution fusion | flops 4023909120 | bytes 11444228 | tf_op jit(solution)/shard_map/while/body/eval_jaxpr/dot_general | solution.py:45
  133.6 12.6 %fusion.102 = bf16[5456,2048]{1,0:T(8,128)(2,1)} fusion(bf16[5456,2048]{1,0:T(8,128)(2,1)} %get-tuple-element.283, s32[]{:T(128)S(6)} %select_n.104, f32[512,5456]{0,1:T(8,128)S(1)} %fusion.100, f32[512,5456]{0,1:T(8,128)S(1)} %fusion.101, s32[5456]{0:T(1024)S(1)} %get-tuple-element.297, f32[120,2048]{1,0:T(8,128)S(1)} %get-tuple-element.294), kind=kOutput, calls=%fused_computation.13.clone.1 | convolution fusion | flops 4032289536 | bytes 28206080 | tf_op jit(solution)/shard_map/while/body/eval_jaxpr/dot_general | solution.py:46
  146.2 10.9 %convolution_bitcast_fusion = f32[32,5456]{1,0:T(8,128)S(1)} fusion(bf16[5456,2048]{1,0:T(8,128)(2,1)} %get-tuple-element.157, f32[32,2048]{1,0:T(8,128)S(1)} %copy-done), kind=kOutput, calls=%fused_computation.31 | convolution fusion | flops 715194368 | bytes 23308288 | tf_op jit(solution)/shard_map/dot_general | solution.py:76
  157.1 0.9 pad_maximum_fusion.2
  158.2 0.6 gather_fusion.2
  158.8 0.6 gather_fusion.1
  162.7 41.9 %psum.29 = f32[3,3]{0,1:T(4,128)S(1)} all-reduce(f32[3,3]{0,1:T(4,128)S(1)} %fusion.72), channel_id=1, replica_groups=mesh['samp'=32] {'samp'}, use_global_device_ids=true, to_apply=%region_9.11 | all-reduce | flops 9 | bytes 72 | tf_op jit(solution)/shard_map/psum | solution.py:61
  209.3 0.7 compare_reduce_fusion.1
  210.1 0.7 fusion.63
  211.9 78.0 %all-reduce.5.cloned.1.call-done = f32[32,5457]{1,0:T(8,128)} async-done(((f32[32,5457]{1,0:T(8,128)}), f32[32,5457]{1,0:T(8,128)}) %all-reduce.5.cloned.1.call-update) | async-done | bytes 698512 | tf_op jit(solution)/shard_map/psum | solution.py:81
  289.9 0.9 fusion.51
  290.8 2.2 divide_bitcast_fusion.2
  293.6 11.0 %fusion.31 = f32[32,5456]{1,0:T(8,128)S(1)} fusion(bf16[5456,2048]{1,0:T(8,128)(2,1)} %get-tuple-element.157, f32[32,2048]{1,0:T(8,128)S(1)} %copy-done, f32[2048]{0:T(1024)S(1)} %bitcast.87, f32[32]{0:T(128)S(1)} %get-tuple-element.196, f32[32]{0:T(128)S(1)} %get-tuple-element.197), kind=kOutput, calls=%fused_computation.66 | convolution fusion | flops 715390976 | bytes 23316736 | tf_op jit(solution)/shard_map/dot_general | solution.py:76
  304.6 0.9 pad_maximum_fusion.3
  308.1 126.6 %all-reduce.7.cloned.1.call-done = f32[32,5457]{1,0:T(8,128)} async-done(((f32[32,5457]{1,0:T(8,128)}), f32[32,5457]{1,0:T(8,128)}) %all-reduce.7.cloned.1.call-update) | async-done | bytes 698512 | tf_op jit(solution)/shard_map/psum | solution.py:81
  434.8 0.9 fusion.47
  435.7 2.4 divide_bitcast_fusion.1
  438.2 2.3 copy.31
  440.5 0.9 fusion.54
  442.9 10.9 %fusion.33 = f32[32,5456]{1,0:T(8,128)S(1)} fusion(bf16[5456,2048]{1,0:T(8,128)(2,1)} %get-tuple-element.157, f32[32,2048]{1,0:T(8,128)S(1)} %get-tuple-element.226), kind=kOutput, calls=%fused_computation.67 | convolution fusion | flops 715194368 | bytes 23308288 | tf_op jit(solution)/shard_map/dot_general | solution.py:76
  453.8 0.9 pad_maximum_fusion.4
  456.1 0.6 compare_reduce_fusion
  456.7 0.6 fusion.57
  458.3 125.6 %all-reduce.9.cloned.1.call-done = f32[32,5457]{1,0:T(8,128)} async-done(((f32[32,5457]{1,0:T(8,128)}), f32[32,5457]{1,0:T(8,128)}) %all-reduce.9.cloned.1.call-update) | async-done | bytes 698512 | tf_op jit(solution)/shard_map/psum | solution.py:81
  583.9 0.9 fusion.43
  584.8 2.4 divide_bitcast_fusion
  587.3 2.3 copy.36
  589.6 0.9 fusion.55
  591.3 0.7 multiply_add_fusion
  592.0 1.1 fusion.22
  593.0 3.0 pad_maximum_fusion
  (68 shorter events, 9.5 us)
Async XLA Ops:
  7.2 282.7 %all-reduce.5.cloned.1.call-start = ((), (), s32[]{:S(2)}) async-start(), calls=%async_computation | async-start | bytes 1409024 | tf_op jit(solution)/shard_map/psum | solution.py:81
  21.8 124.4 %copy-start = (f32[32,2048]{1,0:T(8,128)S(1)}, f32[32,2048]{1,0:T(8,128)}, u32[]{:S(2)}) copy-start(f32[32,2048]{1,0:T(8,128)} %param.17) | copy-start | bytes 786436
  146.2 11.9 %copy-start.1 = (s32[3]{0:T(128)S(1)}, s32[3]{0:T(128)}, u32[]{:S(2)}) copy-start(s32[3]{0:T(128)} %param.19) | copy-start | bytes 40
  158.1 276.7 %all-reduce.7.cloned.1.call-start = ((), (), s32[]{:S(2)}) async-start(), calls=%async_computation.1 | async-start | bytes 1409024 | tf_op jit(solution)/shard_map/psum | solution.py:81
  305.6 278.3 %all-reduce.9.cloned.1.call-start = ((), (), s32[]{:S(2)}) async-start(), calls=%async_computation.2 | async-start | bytes 1409024 | tf_op jit(solution)/shard_map/psum | solution.py:81
Sparse Core Ops, SparseCore 0:
  158.2 131.6 all-reduce.4
  305.7 128.9 all-reduce.6
  454.9 128.9 all-reduce.8
where the time goes:
time: 603 us
  waiting for transfers between devices  330 us (55%)
  matrix products  160 us (27%)
  blocking collectives  41.9 us (7%)
  other arithmetic  27.5 us (5%)
  between operations  22.7 us (4%)
  local copies, waits for them, and re-layouts  20 us (3%)
    psum x3, waiting for transfers between devices, on_device(): total = lax.psum(packed, 'samp')  330 us
    dot_general x4, matrix products, design_select(): third = jnp.dot(picks[2], piece, precision=lax.Precision.HIGHEST)  50.3 us
    psum x1, blocking collectives, on_device(): gram = lax.psum(gram_local, 'samp')  41.9 us
    dot_general x4, matrix products, design_select(): second = jnp.dot(picks[1], piece, precision=lax.Precision.HIGHEST)  37 us
    dot_general x4, matrix products, design_select(): first = jnp.dot(picks[0], piece, precision=lax.Precision.HIGHEST)  37 us
    dot_general x3, matrix products, on_device(): lax.dot_general(rb, basis, (((1,), (1,)), ((), ())), preferred_element_ty...  32.8 us
  transfers between devices with their start and end apart: 3, of which 3 were waited for; matrix products, arithmetic and copies ran while one was open for 2% of the time, Pallas kernels for 0%

commit v1 on v0

v1 whole, which is shorter than its diff:
```python
import functools
import math

import jax
import jax.numpy as jnp
from jax import lax
from jax.experimental import pallas as pl
from jax.experimental.pallas import tpu as pltpu
from jax.sharding import PartitionSpec as P

TILE = 512
NT = (((1,), (1,)), ((), ()))


def up(n, m):
    return -(-n // m) * m


def slots(multi, stride):
    degree = multi.astype(jnp.float32)
    var = lax.broadcasted_iota(jnp.int32, multi.shape, 1).astype(jnp.float32)
    positive = degree > 0.0
    code = degree * float(stride) + var
    count = jnp.sum(jnp.where(positive, 1.0, 0.0), axis=1, keepdims=True)
    total = jnp.sum(jnp.where(positive, code, 0.0), axis=1, keepdims=True)
    high = jnp.max(jnp.where(positive, code, 0.0), axis=1, keepdims=True)
    low = jnp.min(jnp.where(positive, code, 1e6), axis=1, keepdims=True)
    low = jnp.where(count > 0.5, low, 0.0)
    second = jnp.where(count > 1.5, high, 0.0)
    third = jnp.where(count > 2.5, total - low - high, 0.0)
    return low, second, third


def picks(multi, stride):
    levels = 4 * stride
    column = lax.broadcasted_iota(jnp.int32, (multi.shape[0], 2 * levels), 1)
    column = jnp.where(column >= levels, column - levels, column).astype(jnp.float32)
    return jnp.concatenate(
        [jnp.where(column == s, 1.0, 0.0) for s in slots(multi, stride)], axis=0
    ).astype(jnp.bfloat16)


def product(onehot, table):
    rows = onehot.shape[0] // 3
    f = jnp.dot(onehot, table, preferred_element_type=jnp.float32)
    return (f[:rows] * f[rows : 2 * rows] * f[2 * rows :]).astype(jnp.bfloat16)


def split(x):
    high = x.astype(jnp.bfloat16)
    return high, (x - high.astype(jnp.float32)).astype(jnp.bfloat16)


def correlate(cands, stride, chunk, x_ref, res_ref, few_ref, multi_ref, out_ref, active_ref, table, rows):
    step = pl.program_id(0)
    resp, width = res_ref.shape
    levels = 4 * stride
    chunks = [slice(i, i + chunk) for i in range(0, width, chunk)]

    @pl.when(step == 0)
    def _():
        x = x_ref[...]
        second = (3.0 * x * x - 1.0) * 0.5
        third = (5.0 * x * x * x - 3.0 * x) * 0.5
        values = [jnp.ones_like(x), x * math.sqrt(3.0), second * math.sqrt(5.0), third * math.sqrt(7.0)]
        for d, value in enumerate(values):
            high, low = split(value)
            table[d * stride : (d + 1) * stride, :] = high
            table[levels + d * stride : levels + (d + 1) * stride, :] = low
        high, low = split(res_ref[...])
        rows[0:resp, :] = high
        rows[resp : 2 * resp, :] = low
        onehot = picks(few_ref[...], stride)
        for c in chunks:
            active = product(onehot, table[:, c])
            rows[2 * resp :, c] = active
            active_ref[:, c] = active

    onehot = picks(multi_ref[...], stride)
    acc = jnp.zeros((multi_ref.shape[0], rows.shape[0]), jnp.float32)
    for c in chunks:
        psi = product(onehot, table[:, c])
        acc += lax.dot_general(psi, rows[:, c], NT, preferred_element_type=jnp.float32)
    turned = acc.T
    out_ref[0:resp, :] = turned[0:resp] + turned[resp : 2 * resp]
    out_ref[resp:, :] = turned[2 * resp : 2 * resp + out_ref.shape[0] - resp]

    @pl.when(step == pl.num_programs(0) - 1)
    def _():
        res = res_ref[...]
        sq = jnp.sum(res * res, axis=1, keepdims=True)
        tail = out_ref[0:resp, TILE - 128 :]
        lane = lax.broadcasted_iota(jnp.int32, tail.shape, 1)
        out_ref[0:resp, TILE - 128 :] = jnp.where(lane == 127, sq, tail)


def finish(cands, samples, iters, chosen_ref, total_ref, res_ref, active_ref, out_ref, corr_ref, coef_ref):
    resp = res_ref.shape[0]
    total = total_ref[...]
    column = lax.broadcasted_iota(jnp.int32, total.shape, 1)
    picked = [
        jnp.sum(jnp.where(column == chosen_ref[i], total, 0.0), axis=1, keepdims=True)
        for i in range(iters)
    ]
    target = [p[0:resp] for p in picked]
    gram = [[picked[j][resp + i : resp + i + 1] for j in range(iters)] for i in range(iters)]
    sq = total[0:resp, total.shape[1] - 1 :]
    tri = [[None] * iters for _ in range(iters)]
    for i in range(iters):
        for j in range(i + 1):
            s = gram[i][j]
            for m in range(j):
                s = s - tri[i][m] * tri[j][m]
            tri[i][j] = jnp.sqrt(s) if i == j else s / tri[j][j]
    corr = total[0:resp, 0:cands]
    rows = [total[resp + i : resp + i + 1, 0:cands] for i in range(iters)]
    coef = [jnp.zeros((resp, 1), jnp.float32) for _ in range(iters)]
    for k in range(iters):
        norm = math.sqrt(samples) * jnp.sqrt(sq / samples + 1e-06)
        corr_ref[k] = corr * (1.0 / norm)
        largest = jnp.max(jnp.abs(corr), axis=1, keepdims=True)
        gamma = jnp.abs(target[k]) / (largest + 1e-06)
        w = []
        for i in range(k + 1):
            s = target[i]
            for m in range(i):
                s = s - tri[i][m] * w[m]
            w.append(s / tri[i][i])
        for i in reversed(range(k + 1)):
            s = w[i]
            for m in range(i + 1, k + 1):
                s = s - tri[m][i] * w[m]
            w[i] = s / tri[i][i]
        step = [gamma * wi for wi in w]
        for i in range(k + 1):
            coef[i] = coef[i] + step[i]
        if k < iters - 1:
            gain = sum(wi * t for wi, t in zip(w, target))
            sq = jnp.maximum(sq - gamma * (2.0 - gamma) * gain, 0.0)
            target = [
                target[j] - sum(step[i] * gram[i][j] for i in range(k + 1)) for j in range(iters)
            ]
            for i in range(k + 1):
                corr = corr - step[i] * rows[i]
    res = res_ref[...]
    active = active_ref[...].astype(jnp.float32)
    for i in range(iters):
        res = res - coef[i] * active[i : i + 1]
    out_ref[...] = res
    shape = (resp, resp)
    eye = lax.broadcasted_iota(jnp.int32, shape, 0) == lax.broadcasted_iota(jnp.int32, shape, 1)
    lines = [jnp.sum(jnp.where(eye, c, 0.0), axis=0, keepdims=True) for c in coef]
    line = lax.broadcasted_iota(jnp.int32, coef_ref.shape, 0)
    coef_ref[...] = sum(jnp.where(line == i, lines[i], 0.0) for i in range(iters))


def on_device(inputs, response, multi_index, chosen):
    nvars, width = inputs.shape
    samples = width * lax.axis_size("samp")
    cands = multi_index.shape[0]
    iters = chosen.shape[0]
    resp = response.shape[0]
    stride = up(nvars, 16)
    few = up(iters, 16)
    extra = up(iters, 8)
    padded = up(cands + 1, TILE)
    chunk = math.gcd(width, 256)
    x = jnp.pad(inputs, ((0, stride - nvars), (0, 0)))
    picked = jnp.pad(multi_index[chosen], ((0, few - iters), (0, 0)))
    whole = lambda shape: pl.BlockSpec(shape, lambda i: (0, 0))
    local, active = pl.pallas_call(
        functools.partial(correlate, cands, stride, chunk),
        grid=(padded // TILE,),
        in_specs=[
            whole((stride, width)),
            whole((resp, width)),
            whole((few, nvars)),
            pl.BlockSpec((TILE, nvars), lambda i: (i, 0)),
        ],
        out_specs=[pl.BlockSpec((resp + extra, TILE), lambda i: (0, i)), whole((few, width))],
        out_shape=[
            jax.ShapeDtypeStruct((resp + extra, padded), jnp.float32),
            jax.ShapeDtypeStruct((few, width), jnp.bfloat16),
        ],
        scratch_shapes=[
            pltpu.VMEM((8 * stride, width), jnp.bfloat16),
            pltpu.VMEM((2 * resp + few, width), jnp.bfloat16),
        ],
        compiler_params=pltpu.CompilerParams(
            dimension_semantics=("arbitrary",), vmem_limit_bytes=48 * 2**20
        ),
        name="correlate",
    )(x, response, picked, jnp.pad(multi_index, ((0, padded - cands), (0, 0))))
    total = lax.psum(local, "samp")
    vmem = pl.BlockSpec(memory_space=pltpu.VMEM)
    residual, corr, coef = pl.pallas_call(
        functools.partial(finish, cands, samples, iters),
        in_specs=[pl.BlockSpec(memory_space=pltpu.SMEM), vmem, vmem, vmem],
        out_specs=[vmem, vmem, vmem],
        out_shape=[
            jax.ShapeDtypeStruct((resp, width), jnp.float32),
            jax.ShapeDtypeStruct((iters, resp, cands), jnp.float32),
            jax.ShapeDtypeStruct((extra, resp), jnp.float32),
        ],
        compiler_params=pltpu.CompilerParams(vmem_limit_bytes=48 * 2**20),
        name="finish",
    )(chosen, total, response, active)
    return residual, corr, coef[:iters]


def solution(mesh):
    placed = (P(None, "samp"), P(None, "samp"), P(), P())
    return jax.shard_map(
        on_device,
        mesh=mesh,
        in_specs=placed,
        out_specs=(P(None, "samp"), P(), P()),
        check_vma=False,
    )
```

time: 603 us -> 194 us (0.32)
  waiting for transfers between devices: 330 us -> 133 us
  matrix products: 160 us -> 0 us
  blocking collectives: 41.9 us -> 0 us
  Pallas kernels: 0 us -> 36.4 us
  other arithmetic: 27.5 us -> 0.01 us
  local copies, waits for them, and re-layouts: 20 us -> 10.1 us
  between operations: 22.7 us -> 14.1 us
    psum x3 -> x1, waiting for transfers between devices: 330 us -> 133 us  [on_device(): total = lax.psum(local, 'samp')]
    dot_general x18 -> x0, matrix products: 159 us -> none  [the longest x4 50.3 us: design_select(): third = jnp.dot(picks[2], piece, precision=lax.Precision.HIGHEST)]
    psum x1 -> x0, blocking collectives: 41.9 us -> none  [on_device(): gram = lax.psum(gram_local, 'samp')]
    pallas_call x0 -> x2, Pallas kernels: none -> 36.4 us  [the longest x1 33.5 us: on_device(): pl.pallas_call(functools.partial(correlate, cands, stride, chunk), grid=(...]
    another operation x18 -> x0, other arithmetic: 15.4 us -> none  [the longest x4 10 us: on_device(): return (residual, jnp.stack(outs), coefs)]
    broadcast_in_dim x4 -> x0, local copies, waits for them, and re-layouts: 7.95 us -> none  [the longest x1 7.67 us: on_device(): jnp.zeros((cands, rows), jnp.bfloat16)]
  transfers between devices with their start and end apart: 3 -> 1, of which waited for: 3 -> 1; matrix products, arithmetic and copies ran while one was open for 2% -> 0% of each run, Pallas kernels for 0% -> 0%
where the time goes in v1:
time: 194 us
  waiting for transfers between devices  133 us (69%)
  Pallas kernels  36.4 us (19%)
  between operations  14.1 us (7%)
  local copies, waits for them, and re-layouts  10.1 us (5%)
    psum x1, waiting for transfers between devices, on_device(): total = lax.psum(local, 'samp')  133 us
    pallas_call x1, Pallas kernels, on_device(): pl.pallas_call(functools.partial(correlate, cands, stride, chunk), grid=(...  33.5 us
    unnamed x11, local copies, waits for them, and re-layouts  5.12 us
  transfers between devices with their start and end apart: 1, of which 1 were waited for; matrix products, arithmetic and copies ran while one was open for 0% of the time, Pallas kernels for 0%

profile of v1, /device:TPU:0, one launch (start us, length us, event | category | flops | bytes accessed | tf_op | source)
XLA Modules:
  0.0 193.7 jit_solution(8946656857403624955)
XLA Ops:
  7.2 0.0 copy-start.3
  7.2 0.0 all-reduce.5.cloned.1.call-start
  7.2 3.0 %copy.7 = s32[5456,30]{1,0:T(8,128)} copy(s32[5456,30]{0,1:T(8,128)} %param.6) | data formatting | bytes 1309440 | tf_op args[2]
  10.2 0.0 copy-done.3
  10.3 0.0 copy-start.4
  10.3 0.0 copy-start
  10.3 2.0 %pad.14.multi_ref = s32[5632,30]{1,0:T(8,128)S(1)} pad(s32[5456,30]{1,0:T(8,128)} %copy.7, s32[]{:T(128)} %constant.2.clone.1), padding=0_176x0_0 | pad | bytes 1330564 | tf_op jit(solution)/shard_map/jit(_pad)/pad | solution.py:193
  12.3 2.3 %gather_fusion = s32[3,30]{1,0:T(4,128)S(1)} fusion(s32[5456,30]{1,0:T(8,128)} %copy.7, s32[1024]{0:T(1024)S(1)} %pad_clamp_fusion), kind=kCustom, calls=%fused_computation | custom fusion | bytes 732 | tf_op jit(solution)/shard_map/gather | solution.py:169
  14.7 0.0 copy-done.4
  14.7 0.0 copy-done
  14.7 33.5 %correlate.1 = (f32[40,5632]{1,0:T(8,128)S(1)}, bf16[16,2048]{1,0:T(8,128)(2,1)S(1)}) custom-call(f32[32,2048]{1,0:T(8,128)S(1)} %pad.12.x_ref, f32[32,2048]{1,0:T(8,128)S(1)} %copy-done, s32[16,30]{1,0:T(8,128)S(1)} %pad.13.few_ref, s32[5632,30]{1,0:T(8,128)S(1)} %pad.14.multi_ref), custom_call_target="tpu_custom_call" | custom-call | tf_op jit(solution)/shard_map/correlate/pallas_call | solution.py:171
  48.2 0.0 copy-start.2
  48.2 0.9 copy-done.2
  49.1 0.0 all-reduce.5.cloned.1.call-update
  49.1 133.0 %all-reduce.5.cloned.1.call-done.total_ref = f32[40,5632]{1,0:T(8,128)} async-done(((f32[40,5632]{1,0:T(8,128)}), f32[40,5632]{1,0:T(8,128)}) %all-reduce.5.cloned.1.call-update) | async-done | bytes 901136 | tf_op jit(solution)/shard_map/psum | solution.py:194
  182.2 0.0 copy-start.1
  182.2 1.2 copy-done.1
  183.4 2.9 %finish.1 = (f32[32,2048]{1,0:T(8,128)}, f32[3,32,5456]{2,1,0:T(8,128)}, f32[8,32]{1,0:T(8,128)S(1)}) custom-call(s32[3]{0:T(128)S(1)} %copy-done.3, f32[40,5632]{1,0:T(8,128)S(1)} %copy-done.1, f32[32,2048]{1,0:T(8,128)S(1)} %copy-done, bf16[16,2048]{1,0:T(8,128)(2,1)S(1)} %get-tuple-element.9.active_ref), custom_call_target="tpu_custom_call" | custom-call | tf_op jit(solution)/shard_map/finish/pallas_call | solution.py:196
  186.3 0.6 slice.3
  (4 shorter events, 0.0 us)
Async XLA Ops:
  7.2 3.1 %copy-start.3 = (s32[3]{0:T(128)S(1)}, s32[3]{0:T(128)}, u32[]{:S(2)}) copy-start(s32[3]{0:T(128)} %chosen_ref.1) | copy-start | bytes 40
  7.2 175.0 %all-reduce.5.cloned.1.call-start = ((), (), s32[]{:S(2)}) async-start(), calls=%async_computation | async-start | bytes 1802240 | tf_op jit(solution)/shard_map/psum | solution.py:194
  10.3 4.4 %copy-start.4 = (f32[30,2048]{1,0:T(8,128)S(1)}, f32[30,2048]{1,0:T(8,128)}, u32[]{:S(2)}) copy-start(f32[30,2048]{1,0:T(8,128)} %param.4) | copy-start | bytes 737284
  10.3 4.4 %copy-start = (f32[32,2048]{1,0:T(8,128)S(1)}, f32[32,2048]{1,0:T(8,128)}, u32[]{:S(2)}) copy-start(f32[32,2048]{1,0:T(8,128)} %res_ref.3) | copy-start | bytes 786436
  48.2 0.9 copy-start.2
  182.2 1.2 copy-start.1
Sparse Core Ops, SparseCore 0:
  49.3 132.8 all-reduce.4
